TPU v7x, 32 devices: a whole 2x2x4 slice. The times are simulated.
32 devices in a mesh: grp: 2 (over y), ctx: 4 (over x, core), head: 4 (over z).
Axes of the slice: x: 2, y: 2, z: 4, core: 2. Of those that a mesh axis runs over, the one named last changes fastest.
Arguments:
- prompt_hidden: bfloat16 [4, 1024, 4096], P('grp', 'ctx', 'head'), parts along dimension 0, may hold values from -3 to 3
- qkv_weight: bfloat16 [3, 4096, 4096], P(None, 'ctx', 'head'), may hold values from -0.09375 to 0.09375
- out_weight: bfloat16 [4096, 4096], P('head', 'ctx'), may hold values from -0.9375 to 0.9375
- embed_table: bfloat16 [32768, 4096], P('ctx', 'head'), may hold values from -60 to 60
- response_ids: int32 [4, 256], P(None, 'grp'), parts along dimension 1, may hold values from 0 to 32767
- assignment: int32 [256], P('grp'), parts along dimension 0, may hold values from 0 to 1
Outputs:
- final_hidden: bfloat16 [4, 256, 4096], P(None, ('grp', 'ctx'), 'head'), parts along dimension 1
There are 2 independent parts, one for each index of `grp`. A program takes and returns all parts, laid end to end along the dimension named above; an argument that names none is the same for every part. Nothing has to cross between parts.
All inputs are finite; a program needn't handle non-finite values.
Results may differ from a plain program's by a relative error of at most 0.023.
Values may be sent and summed in bfloat16 or wider, within the bound.
A program may use at most 128 MiB of HBM per device.

v0:
```python
import jax
import jax.numpy as jnp
from jax import lax
from jax.sharding import PartitionSpec as P

DH = 128


def rms_rows(values):
    return values * lax.rsqrt(jnp.mean(values * values, axis=-1, keepdims=True) + 1e-06)


def on_device(prompt_hidden, qkv_weight, out_weight, embed_table, response_ids, assignment):
    local_cols = prompt_hidden.shape[2]
    prompt_rows = prompt_hidden.shape[1]
    head_size = DH
    local_heads = local_cols // head_size
    steps = response_ids.shape[0]
    resp_local = response_ids.shape[1] // lax.axis_size("ctx")
    ctx_index = lax.axis_index("ctx")
    full_rows = lax.all_gather(qkv_weight, "ctx", axis=1, tiled=True)
    kv_weight = jnp.concatenate([full_rows[1], full_rows[2]], axis=1)
    piece = lax.all_gather(prompt_hidden, "head", axis=2, tiled=True)
    flat_piece = piece.reshape(2 * prompt_rows, piece.shape[2])
    kv_local = jnp.dot(flat_piece, kv_weight, preferred_element_type=jnp.float32)
    kv_local = kv_local.astype(jnp.bfloat16).reshape(2, prompt_rows, 2, local_heads, head_size)
    partial_state = jnp.einsum(
        "pthd,pthe->phde", kv_local[:, :, 0], kv_local[:, :, 1], preferred_element_type=jnp.float32
    )
    state = lax.psum(partial_state.astype(jnp.bfloat16), "ctx").astype(jnp.float32)
    vocab_rows = embed_table.shape[0]
    offset_ids = response_ids - ctx_index * vocab_rows
    inside = (offset_ids >= 0) & (offset_ids < vocab_rows)
    looked = jnp.take(embed_table, jnp.clip(offset_ids, 0, vocab_rows - 1), axis=0)
    looked = jnp.where(inside[:, :, None], looked.astype(jnp.float32), 0.0)
    embedded_mine = lax.psum_scatter(
        looked.astype(jnp.bfloat16), "ctx", scatter_dimension=1, tiled=True
    )
    embedded = lax.all_gather(embedded_mine, "head", axis=2, tiled=True)
    normed = rms_rows(embedded.astype(jnp.float32)).astype(jnp.bfloat16)
    projected_qkv = jnp.einsum(
        "trd,kde->trke", normed, full_rows, preferred_element_type=jnp.float32
    ).astype(jnp.bfloat16)
    projected_qkv = projected_qkv.reshape(steps, resp_local, 3, local_heads, head_size)
    query = projected_qkv[:, :, 0]
    key = projected_qkv[:, :, 1]
    value = projected_qkv[:, :, 2]
    my_prompt = lax.dynamic_slice_in_dim(assignment, ctx_index * resp_local, resp_local, 0)
    query_f = query.astype(jnp.float32)
    both = jnp.einsum("trhd,phde->ptrhe", query_f, state, precision=lax.Precision.HIGHEST)
    chosen = jnp.where((my_prompt == 0)[None, :, None, None], both[0], both[1])
    scores = jnp.einsum("trhd,srhd->rhts", query, key, preferred_element_type=jnp.float32)
    later = jnp.arange(steps)[:, None] >= jnp.arange(steps)[None, :]
    scores = jnp.where(later[None, None], scores, 0.0).astype(jnp.bfloat16)
    local = jnp.einsum("rhts,srhd->trhd", scores, value, preferred_element_type=jnp.float32)
    head_out = rms_rows(chosen + local).astype(jnp.bfloat16).reshape(steps, resp_local, local_cols)
    terms = jnp.einsum(
        "trd,de->tre",
        head_out,
        lax.all_gather(out_weight, "ctx", axis=1, tiled=True),
        preferred_element_type=jnp.float32,
    )
    width = terms.shape[2]
    mine = lax.psum_scatter(
        terms.astype(jnp.bfloat16), "head", scatter_dimension=2, tiled=True
    ).astype(jnp.float32)
    mixed = embedded_mine.astype(jnp.float32) + mine
    squares = lax.psum(jnp.sum(mixed * mixed, axis=-1), "head")
    result = mixed * lax.rsqrt(squares[:, :, None] / width + 1e-06)
    return result.astype(jnp.bfloat16)


def solution(mesh):
    return jax.shard_map(
        on_device,
        mesh=mesh,
        in_specs=(
            P("grp", "ctx", "head"),
            P(None, "ctx", "head"),
            P("head", "ctx"),
            P("ctx", "head"),
            P(None, "grp"),
            P("grp"),
        ),
        out_specs=P(None, ("grp", "ctx"), "head"),
        check_vma=False,
    )
```

profile of v0, /device:TPU:0, one launch (start us, length us, event | category | flops | bytes accessed | tf_op | source)
XLA Modules:
  0.0 461.3 jit_solution(4606842393122182999)
XLA Ops:
  6.5 0.0 reduce-scatter.3.cloned.1.call-start
  6.5 0.7 compare_and_fusion.1
  7.2 0.7 fusion.41
  7.9 10.7 %gather_fusion = bf16[512,1024]{1,0:T(8,128)(2,1)S(1)} fusion(bf16[8192,1024]{1,0:T(8,128)(2,1)} %param.9, s32[1024]{0:T(1024)S(1)} %pad_clamp_fusion), kind=kCustom, calls=%fused_computation | custom fusion | bytes 2099200 | tf_op jit(solution)/shard_map/jit(_take)/gather | solution.py:34
  18.6 1.4 select_convert_fusion
  20.0 0.0 reduce-scatter.3.cloned.1.call-update
  20.0 0.0 all-gather.5.cloned.1.call-start
  20.0 0.7 all-gather.5.cloned.1.call-update
  20.7 0.0 all-gather.7.cloned.1.call-start
  20.8 0.7 all-gather.7.cloned.1.call-update
  21.5 0.0 all-gather.9.cloned.1.call-start
  21.5 26.1 %reduce-scatter.3.cloned.1.call-done = bf16[4,32,1024]{2,1,0:T(8,128)(2,1)} async-done(((bf16[4,128,1024]{2,1,0:T(8,128)(2,1)}), bf16[4,32,1024]{2,1,0:T(8,128)(2,1)}) %reduce-scatter.3.cloned.1.call-update) | async-done | bytes 262160 | tf_op jit(solution)/shard_map/reduce_scatter | solution.py:36
  47.7 0.0 all-gather.9.cloned.1.call-update
  47.7 0.2 all-reduce.2.cloned.1.call-start
  47.9 156.1 %all-gather.5.cloned.1.call-done = bf16[3,4096,1024]{2,1,0:T(8,128)(2,1)} async-done(((bf16[3,1024,1024]{2,1,0:T(8,128)(2,1)}), bf16[3,4096,1024]{2,1,0:T(8,128)(2,1)}) %all-gather.5.cloned.1.call-update) | async-done | bytes 25165840 | tf_op jit(solution)/shard_map/all_gather | solution.py:21
  204.0 11.8 %slice_bitcast_fusion.1 = (bf16[4096,1024]{1,0:T(8,128)(2,1)}, bf16[4096,1024]{1,0:T(8,128)(2,1)}) fusion(bf16[3,4096,1024]{2,1,0:T(8,128)(2,1)} %all-gather.5.cloned.1.call-done), kind=kLoop, calls=%fused_computation.8 | loop fusion | bytes 33554432 | tf_op jit(solution)/shard_map/squeeze | solution.py:22
  215.9 70.5 %all-gather.7.cloned.1.call-done = bf16[2,256,4096]{2,1,0:T(8,128)(2,1)} async-done(((bf16[2,256,1024]{2,1,0:T(8,128)(2,1)}), bf16[2,256,4096]{2,1,0:T(8,128)(2,1)}) %all-gather.7.cloned.1.call-update) | async-done | bytes 4194320 | tf_op jit(solution)/shard_map/all_gather | solution.py:23
  286.4 17.3 %fusion.14 = bf16[512,2048]{0,1:T(8,128)(2,1)} fusion(bf16[512,4096]{1,0:T(8,128)(2,1)} %bitcast.86, bf16[4096,1024]{1,0:T(8,128)(2,1)} %get-tuple-element.8, bf16[4096,1024]{1,0:T(8,128)(2,1)} %get-tuple-element.7), kind=kOutput, calls=%fused_computation.13 | convolution fusion | flops 8624537600 | bytes 23068672 | tf_op jit(solution)/shard_map/dot_general | solution.py:25
  303.7 0.0 copy-start.1
  303.7 2.6 reshape.52
  306.3 1.5 slice_bitcast_fusion.3
  307.8 1.3 convolution_convert_fusion
  309.1 0.0 all-reduce.2.cloned.1.call-update
  309.1 0.0 all-gather.11.cloned.1.call-start
  309.1 0.5 all-gather.11.cloned.1.call-update
  309.7 0.3 reduce-scatter.5.cloned.1.call-start
  310.0 0.0 copy-done.1
  310.0 0.1 dynamic-slice_compare_fusion
  310.0 4.3 all-gather.9.cloned.1.call-done
  314.3 1.5 fusion.17
  315.9 12.1 %fusion.19 = bf16[4,32,3,1024]{3,1,2,0:T(8,128)(2,1)S(1)} fusion(bf16[3,4096,1024]{2,1,0:T(8,128)(2,1)} %all-gather.5.cloned.1.call-done, bf16[4,32,4096]{2,1,0:T(8,128)(2,1)} %all-gather.9.cloned.1.call-done, f32[4,32]{1,0:T(4,128)S(1)} %add_rsqrt_fusion.2), kind=kOutput, calls=%fused_computation.19 | convolution fusion | flops 3223191552 | bytes 27001344 | tf_op jit(solution)/shard_map/trd,kde->trke/dot_general | solution.py:41
  327.9 0.2 copy.28
  328.1 0.2 fusion.45
  328.3 0.7 fusion.23
  329.0 0.0 copy-start
  329.0 20.3 %all-reduce.2.cloned.1.call-done = bf16[2,8,128,128]{3,2,0,1:T(8,128)(2,1)} async-done(((bf16[2,8,128,128]{3,2,0,1:T(8,128)(2,1)}), bf16[2,8,128,128]{3,2,0,1:T(8,128)(2,1)}) %all-reduce.2.cloned.1.call-update) | async-done | bytes 524304 | tf_op jit(solution)/shard_map/psum | solution.py:30
  349.3 1.3 convolution_bitcast_fusion
  350.7 0.4 multiply_reduce_fusion.1
  351.1 58.0 %all-gather.11.cloned.1.call-done = bf16[1024,4096]{1,0:T(8,128)(2,1)} async-done(((bf16[1024,1024]{1,0:T(8,128)(2,1)}), bf16[1024,4096]{1,0:T(8,128)(2,1)}) %all-gather.11.cloned.1.call-update) | async-done | bytes 8388624 | tf_op jit(solution)/shard_map/all_gather | solution.py:60
  409.2 5.7 %fusion.8 = bf16[4,32,4096]{2,1,0:T(8,128)(2,1)} fusion(bf16[1024,4096]{1,0:T(8,128)(2,1)} %all-gather.11.cloned.1.call-done, f32[4,32,8,128]{3,1,0,2:T(8,128)S(1)} %get-tuple-element.6, f32[4,32,8]{1,0,2:T(4,128)S(1)} %add_rsqrt_fusion), kind=kOutput, calls=%fused_computation.11 | convolution fusion | flops 1074528256 | bytes 9965568 | tf_op jit(solution)/shard_map/trd,de->tre/dot_general | solution.py:57
  414.8 0.0 reduce-scatter.5.cloned.1.call-update
  414.9 27.4 %reduce-scatter.5.cloned.1.call-done = bf16[4,32,1024]{2,1,0:T(8,128)(2,1)} async-done(((bf16[4,32,4096]{2,1,0:T(8,128)(2,1)}), bf16[4,32,1024]{2,1,0:T(8,128)(2,1)}) %reduce-scatter.5.cloned.1.call-update) | async-done | bytes 262160 | tf_op jit(solution)/shard_map/reduce_scatter | solution.py:64
  442.3 0.0 copy-done
  442.3 1.1 multiply_reduce_fusion
  443.4 9.3 %psum.15 = f32[4,32]{1,0:T(4,128)S(1)} all-reduce(f32[4,32]{1,0:T(4,128)S(1)} %multiply_reduce_fusion), channel_id=1, replica_groups=mesh['grp'=2,'ctx'=4,'head'=4] {'head'}, use_global_device_ids=true, to_apply=%region_6.7 | all-reduce | flops 128 | bytes 1024 | tf_op jit(solution)/shard_map/psum | solution.py:68
  452.7 1.8 multiply_convert_fusion
  (5 shorter events, 0.0 us)
Async XLA Ops:
  6.5 41.1 %reduce-scatter.3.cloned.1.call-start = ((), (), s32[]{:S(2)}) async-start(), calls=%async_computation.2 | async-start | bytes 1310720 | tf_op jit(solution)/shard_map/reduce_scatter | solution.py:36
  20.0 184.1 %all-gather.5.cloned.1.call-start = ((), (), s32[]{:S(2)}) async-start(), calls=%async_computation.3 | async-start | bytes 31457280 | tf_op jit(solution)/shard_map/all_gather | solution.py:21
  20.7 265.7 %all-gather.7.cloned.1.call-start = ((), (), s32[]{:S(2)}) async-start(), calls=%async_computation.4 | async-start | bytes 5242880 | tf_op jit(solution)/shard_map/all_gather | solution.py:23
  21.5 292.8 %all-gather.9.cloned.1.call-start = ((), (), s32[]{:S(2)}) async-start(), calls=%async_computation.6 | async-start | bytes 1310720 | tf_op jit(solution)/shard_map/all_gather | solution.py:39
  47.7 301.7 %all-reduce.2.cloned.1.call-start = ((), (), s32[]{:S(2)}) async-start(), calls=%async_computation.5 | async-start | bytes 1048576 | tf_op jit(solution)/shard_map/psum | solution.py:30
  303.7 6.2 %copy-start.1 = (s32[128]{0:T(128)S(1)}, s32[128]{0:T(128)}, u32[]{:S(2)}) copy-start(s32[128]{0:T(128)} %param.11) | copy-start | bytes 1540
  309.1 100.1 %all-gather.11.cloned.1.call-start = ((), (), s32[]{:S(2)}) async-start(), calls=%async_computation.7 | async-start | bytes 10485760 | tf_op jit(solution)/shard_map/all_gather | solution.py:60
  309.7 132.6 %reduce-scatter.5.cloned.1.call-start = ((), (), s32[]{:S(2)}) async-start(), calls=%async_computation.8 | async-start | bytes 1310720 | tf_op jit(solution)/shard_map/reduce_scatter | solution.py:64
  329.0 113.3 %copy-start = (bf16[4,32,1024]{2,1,0:T(8,128)(2,1)S(1)}, bf16[4,32,1024]{2,1,0:T(8,128)(2,1)}, u32[]{:S(2)}) copy-start(bf16[4,32,1024]{2,1,0:T(8,128)(2,1)} %reduce-scatter.3.cloned.1.call-done) | copy-start | bytes 786436
Sparse Core Ops, SparseCore 0:
  20.1 27.4 reduce-scatter.2
  49.2 154.7 all-gather.4
  205.6 80.7 all-gather.6
  287.8 26.4 all-gather.8
  316.5 32.7 all-reduce.1
  350.8 58.3 all-gather.10
  415.0 27.2 reduce-scatter.4
where the time goes:
time: 462 us; the launch traced here: 461 us
  waiting for transfers between devices  365 us (79%)
  matrix products  38.4 us (8%)
  local copies, waits for them, and re-layouts  26.9 us (6%)
  between operations  13.6 us (3%)
  blocking collectives  9.28 us (2%)
  other arithmetic  7.7 us (2%)
    all_gather x1, waiting for transfers between devices, on_device(): full_rows = lax.all_gather(qkv_weight, 'ctx', axis=1, tiled=True)  156 us
    all_gather x1, waiting for transfers between devices, on_device(): piece = lax.all_gather(prompt_hidden, 'head', axis=2, tiled=True)  70.5 us
    all_gather x1, waiting for transfers between devices, on_device(): lax.all_gather(out_weight, 'ctx', axis=1, tiled=True)  58 us
    reduce_scatter x1, waiting for transfers between devices, on_device(): lax.psum_scatter(terms.astype(jnp.bfloat16), 'head', scatter_dimension=2,...  27.4 us
    reduce_scatter x1, waiting for transfers between devices, on_device(): lax.psum_scatter(looked.astype(jnp.bfloat16), 'ctx', scatter_dimension=1,...  26.1 us
    psum x1, waiting for transfers between devices, on_device(): lax.psum(partial_state.astype(jnp.bfloat16), 'ctx').astype(jnp.float32)  20.3 us
    dot_general x1, matrix products, on_device(): jnp.dot(flat_piece, kv_weight, preferred_element_type=jnp.float32)  17.3 us
    dot_general x1, matrix products, on_device(): jnp.einsum('trd,kde->trke', normed, full_rows, preferred_element_type=jnp...  12.1 us
  transfers between devices with their start and end apart: 7, of which 7 were waited for; matrix products, arithmetic and copies ran while one was open for 11% of the time, Pallas kernels for 0%

commit v1 on v0

--- a/solution.py
+++ b/solution.py
@@ -54,12 +54,18 @@
     scores = jnp.where(later[None, None], scores, 0.0).astype(jnp.bfloat16)
     local = jnp.einsum("rhts,srhd->trhd", scores, value, preferred_element_type=jnp.float32)
     head_out = rms_rows(chosen + local).astype(jnp.bfloat16).reshape(steps, resp_local, local_cols)
-    terms = jnp.einsum(
-        "trd,de->tre",
-        head_out,
-        lax.all_gather(out_weight, "ctx", axis=1, tiled=True),
-        preferred_element_type=jnp.float32,
-    )
+    size, index, rows = (lax.axis_size("ctx"), lax.axis_index("ctx"), out_weight.shape[1])
+    right = [(i, (i + 1) % size) for i in range(size)]
+    block, terms = (out_weight, None)
+    for step in range(size):
+        source = (index - step) % size
+        arriving = lax.ppermute(block, "ctx", right) if step < size - 1 else None
+        made = jnp.einsum("trd,de->tre", head_out, block, preferred_element_type=jnp.float32)
+        length = made.shape[2]
+        if terms is None:
+            terms = jnp.zeros((*made.shape[:2], size * length, *made.shape[2 + 1 :]), made.dtype)
+        terms = lax.dynamic_update_slice_in_dim(terms, made, source * length, axis=2)
+        block = arriving
     width = terms.shape[2]
     mine = lax.psum_scatter(
         terms.astype(jnp.bfloat16), "head", scatter_dimension=2, tiled=True

time: 462 us -> 455 us (0.985)
  waiting for transfers between devices: 365 us -> 355 us
    all_gather x1 -> x0, waiting for transfers between devices: 58 us -> none  [on_device(): lax.all_gather(out_weight, 'ctx', axis=1, tiled=True)]
    ppermute x0 -> x3, waiting for transfers between devices: none -> 56.8 us  [on_device(): arriving = lax.ppermute(block, 'ctx', right) if step < size - 1 else None]
    all_gather x1, waiting for transfers between devices: 70.5 us -> 58.4 us  [on_device(): piece = lax.all_gather(prompt_hidden, 'head', axis=2, tiled=True)]
    psum x1, waiting for transfers between devices: 20.3 us -> 30.9 us  [on_device(): lax.psum(partial_state.astype(jnp.bfloat16), 'ctx').astype(jnp.float32)]
    all_gather x1, waiting for transfers between devices: 156 us -> 150 us  [on_device(): full_rows = lax.all_gather(qkv_weight, 'ctx', axis=1, tiled=True)]
  transfers between devices with their start and end apart: 7 -> 9, of which waited for: 7 -> 8; matrix products, arithmetic and copies ran while one was open for 11% -> 12% of each run, Pallas kernels for 0% -> 0%
where the time goes in v1:
time: 455 us; the launch traced here: 454 us
  waiting for transfers between devices  355 us (78%)
  matrix products  38.9 us (9%)
  local copies, waits for them, and re-layouts  29.6 us (7%)
  between operations  13.7 us (3%)
  blocking collectives  9.28 us (2%)
  other arithmetic  7.92 us (2%)
    all_gather x1, waiting for transfers between devices, on_device(): full_rows = lax.all_gather(qkv_weight, 'ctx', axis=1, tiled=True)  150 us
    all_gather x1, waiting for transfers between devices, on_device(): piece = lax.all_gather(prompt_hidden, 'head', axis=2, tiled=True)  58.4 us
    ppermute x3, waiting for transfers between devices, on_device(): arriving = lax.ppermute(block, 'ctx', right) if step < size - 1 else None  56.8 us
    psum x1, waiting for transfers between devices, on_device(): lax.psum(partial_state.astype(jnp.bfloat16), 'ctx').astype(jnp.float32)  30.9 us
    reduce_scatter x1, waiting for transfers between devices, on_device(): lax.psum_scatter(looked.astype(jnp.bfloat16), 'ctx', scatter_dimension=1,...  27.6 us
    reduce_scatter x1, waiting for transfers between devices, on_device(): lax.psum_scatter(terms.astype(jnp.bfloat16), 'head', scatter_dimension=2,...  27.6 us
    dot_general x1, matrix products, on_device(): jnp.dot(flat_piece, kv_weight, preferred_element_type=jnp.float32)  17.2 us
    squeeze x1, local copies, waits for them, and re-layouts, on_device(): kv_weight = jnp.concatenate([full_rows[1], full_rows[2]], axis=1)  11.9 us
  transfers between devices with their start and end apart: 9, of which 8 were waited for; matrix products, arithmetic and copies ran while one was open for 12% of the time, Pallas kernels for 0%

profile of v1, /device:TPU:0, one launch (start us, length us, event | category | flops | bytes accessed | tf_op | source)
XLA Modules:
  0.0 454.2 jit_solution(15836116626940498797)
XLA Ops:
  6.5 0.7 compare_and_fusion.1
  7.2 0.7 fusion.62
  7.9 10.7 %gather_fusion = bf16[512,1024]{1,0:T(8,128)(2,1)S(1)} fusion(bf16[8192,1024]{1,0:T(8,128)(2,1)} %param.9, s32[1024]{0:T(1024)S(1)} %pad_clamp_fusion), kind=kCustom, calls=%fused_computation | custom fusion | bytes 2099200 | tf_op jit(solution)/shard_map/jit(_take)/gather | solution.py:34
  18.6 1.3 select_convert_fusion
  19.9 0.0 reduce-scatter.3.cloned.1.call-update
  19.9 0.0 all-gather.8.cloned.1.call-start
  20.0 27.6 %reduce-scatter.3.cloned.1.call-done = bf16[4,32,1024]{2,1,0:T(8,128)(2,1)} async-done(((bf16[4,128,1024]{2,1,0:T(8,128)(2,1)}), bf16[4,32,1024]{2,1,0:T(8,128)(2,1)}) %reduce-scatter.3.cloned.1.call-update) | async-done | bytes 262160 | tf_op jit(solution)/shard_map/reduce_scatter | solution.py:36
  47.6 0.0 all-gather.8.cloned.1.call-update
  47.6 0.0 all-gather.4.cloned.1.call-start
  47.7 0.7 all-gather.4.cloned.1.call-update
  48.4 0.0 all-gather.6.cloned.1.call-start
  48.4 0.8 copy-done.3
  49.2 0.0 all-gather.6.cloned.1.call-update
  49.2 0.0 all-reduce.2.cloned.1.call-start
  49.3 25.5 %collective-permute-done = bf16[1024,1024]{1,0:T(8,128)(2,1)} collective-permute-done((bf16[1024,1024]{1,0:T(8,128)(2,1)S(1)}, bf16[1024,1024]{1,0:T(8,128)(2,1)}, u32[]{:S(2)}, u32[]{:S(2)}) %collective-permute-start) | collective-permute-done | bytes 2097184 | tf_op jit(solution)/shard_map/ppermute | solution.py:62
  74.8 0.1 dynamic-slice_compare_fusion
  74.9 2.3 all-gather.8.cloned.1.call-done
  77.2 1.6 fusion.12
  78.8 31.3 %collective-permute-done.1 = bf16[1024,1024]{1,0:T(8,128)(2,1)} collective-permute-done((bf16[1024,1024]{1,0:T(8,128)(2,1)}, bf16[1024,1024]{1,0:T(8,128)(2,1)}, u32[]{:S(2)}, u32[]{:S(2)}) %collective-permute-start.1) | collective-permute-done | bytes 2097184 | tf_op jit(solution)/shard_map/ppermute | solution.py:62
  110.1 150.2 %all-gather.4.cloned.1.call-done = bf16[3,4096,1024]{2,1,0:T(8,128)(2,1)} async-done(((bf16[3,1024,1024]{2,1,0:T(8,128)(2,1)}), bf16[3,4096,1024]{2,1,0:T(8,128)(2,1)}) %all-gather.4.cloned.1.call-update) | async-done | bytes 25165840 | tf_op jit(solution)/shard_map/all_gather | solution.py:21
  260.3 11.7 %fusion.22 = bf16[4,32,3,1024]{3,1,2,0:T(8,128)(2,1)S(1)} fusion(bf16[3,4096,1024]{2,1,0:T(8,128)(2,1)} %all-gather.4.cloned.1.call-done, bf16[4,32,4096]{2,1,0:T(8,128)(2,1)S(1)} %copy-done, f32[4,32]{1,0:T(4,128)S(1)} %add_rsqrt_fusion.2), kind=kOutput, calls=%fused_computation.24 | convolution fusion | flops 3223191552 | bytes 27001344 | tf_op jit(solution)/shard_map/trd,kde->trke/dot_general | solution.py:41
  272.0 0.2 copy.28
  272.2 11.9 %slice_bitcast_fusion.1 = (bf16[4096,1024]{1,0:T(8,128)(2,1)}, bf16[4096,1024]{1,0:T(8,128)(2,1)}) fusion(bf16[3,4096,1024]{2,1,0:T(8,128)(2,1)} %all-gather.4.cloned.1.call-done), kind=kLoop, calls=%fused_computation.8 | loop fusion | bytes 33554432 | tf_op jit(solution)/shard_map/squeeze | solution.py:22
  284.0 58.4 %all-gather.6.cloned.1.call-done = bf16[2,256,4096]{2,1,0:T(8,128)(2,1)} async-done(((bf16[2,256,1024]{2,1,0:T(8,128)(2,1)}), bf16[2,256,4096]{2,1,0:T(8,128)(2,1)}) %all-gather.6.cloned.1.call-update) | async-done | bytes 4194320 | tf_op jit(solution)/shard_map/all_gather | solution.py:23
  342.5 17.2 %fusion.9 = bf16[512,2048]{0,1:T(8,128)(2,1)} fusion(bf16[512,4096]{1,0:T(8,128)(2,1)} %bitcast.105, bf16[4096,1024]{1,0:T(8,128)(2,1)} %get-tuple-element.8, bf16[4096,1024]{1,0:T(8,128)(2,1)} %get-tuple-element.7), kind=kOutput, calls=%fused_computation.10 | convolution fusion | flops 8624537600 | bytes 23068672 | tf_op jit(solution)/shard_map/dot_general | solution.py:25
  359.7 2.5 reshape.52
  362.3 1.5 slice_bitcast_fusion.3
  363.8 1.2 convolution_convert_fusion
  365.0 0.0 all-reduce.2.cloned.1.call-update
  365.0 0.3 reduce-scatter.5.cloned.1.call-start
  365.3 0.1 fusion.66
  365.4 0.7 fusion.38
  366.2 30.9 %all-reduce.2.cloned.1.call-done = bf16[2,8,128,128]{3,2,0,1:T(8,128)(2,1)} async-done(((bf16[2,8,128,128]{3,2,0,1:T(8,128)(2,1)}), bf16[2,8,128,128]{3,2,0,1:T(8,128)(2,1)}) %all-reduce.2.cloned.1.call-update) | async-done | bytes 524304 | tf_op jit(solution)/shard_map/psum | solution.py:30
  397.1 1.3 convolution_bitcast_fusion
  398.4 0.4 multiply_reduce_fusion.1
  398.9 0.2 fusion.47
  399.1 0.1 broadcast_in_dim.60
  399.2 0.8 copy-done.4
  400.0 0.4 fusion.25
  400.4 2.0 fusion.28
  402.5 2.0 fusion.31
  404.6 2.1 fusion.34
  406.7 1.0 copy-done.1
  407.6 0.0 reduce-scatter.5.cloned.1.call-update
  407.6 27.6 %reduce-scatter.5.cloned.1.call-done = bf16[4,32,1024]{2,1,0:T(8,128)(2,1)} async-done(((bf16[4,32,4096]{2,1,0:T(8,128)(2,1)}), bf16[4,32,1024]{2,1,0:T(8,128)(2,1)}) %reduce-scatter.5.cloned.1.call-update) | async-done | bytes 262160 | tf_op jit(solution)/shard_map/reduce_scatter | solution.py:70
  435.2 1.1 multiply_reduce_fusion
  436.3 9.3 %psum.15 = f32[4,32]{1,0:T(4,128)S(1)} all-reduce(f32[4,32]{1,0:T(4,128)S(1)} %multiply_reduce_fusion), channel_id=1, replica_groups=mesh['grp'=2,'ctx'=4,'head'=4] {'head'}, use_global_device_ids=true, to_apply=%region_6.7 | all-reduce | flops 128 | bytes 1024 | tf_op jit(solution)/shard_map/psum | solution.py:74
  445.6 1.8 multiply_convert_fusion
  (19 shorter events, 0.1 us)
Async XLA Ops:
  6.5 41.0 %reduce-scatter.3.cloned.1.call-start = ((), (), s32[]{:S(2)}) async-start(), calls=%async_computation.2 | async-start | bytes 1310720 | tf_op jit(solution)/shard_map/reduce_scatter | solution.py:36
  19.9 57.3 %all-gather.8.cloned.1.call-start = ((), (), s32[]{:S(2)}) async-start(), calls=%async_computation.6 | async-start | bytes 1310720 | tf_op jit(solution)/shard_map/all_gather | solution.py:39
  47.6 1.6 copy-start.3
  47.6 27.2 %copy-start.5 = (s32[128]{0:T(128)S(1)}, s32[128]{0:T(128)}, u32[]{:S(2)}) copy-start(s32[128]{0:T(128)} %param.11) | copy-start | bytes 1540
  47.6 212.6 %all-gather.4.cloned.1.call-start = ((), (), s32[]{:S(2)}) async-start(), calls=%async_computation.3 | async-start | bytes 31457280 | tf_op jit(solution)/shard_map/all_gather | solution.py:21
  48.4 294.1 %all-gather.6.cloned.1.call-start = ((), (), s32[]{:S(2)}) async-start(), calls=%async_computation.4 | async-start | bytes 5242880 | tf_op jit(solution)/shard_map/all_gather | solution.py:23
  49.2 25.6 %collective-permute-start = (bf16[1024,1024]{1,0:T(8,128)(2,1)S(1)}, bf16[1024,1024]{1,0:T(8,128)(2,1)}, u32[]{:S(2)}, u32[]{:S(2)}) collective-permute-start(bf16[1024,1024]{1,0:T(8,128)(2,1)S(1)} %copy-done.3), channel_id=1, source_target_pairs={{0,4},{4,8},{8,12},{12,0},{1,5},{5,9},{9,13},{13,1},{2,6},{6,10},{... | collective-permute-start | bytes 6291464 | tf_op jit(solution)/shard_map/ppermute | solution.py:62
  49.2 347.8 %all-reduce.2.cloned.1.call-start = ((), (), s32[]{:S(2)}) async-start(), calls=%async_computation.5 | async-start | bytes 1048576 | tf_op jit(solution)/shard_map/psum | solution.py:30
  74.8 35.3 %collective-permute-start.1 = (bf16[1024,1024]{1,0:T(8,128)(2,1)}, bf16[1024,1024]{1,0:T(8,128)(2,1)}, u32[]{:S(2)}, u32[]{:S(2)}) collective-permute-start(bf16[1024,1024]{1,0:T(8,128)(2,1)} %collective-permute-done), channel_id=1, source_target_pairs={{0,4},{4,8},{8,12},{12,0},{1,5},{5,9},{9,13},{13,1},{2,6},{6,10},{... | collective-permute-start | bytes 6291464 | tf_op jit(solution)/shard_map/ppermute | solution.py:62
  77.2 183.1 %copy-start = (bf16[4,32,4096]{2,1,0:T(8,128)(2,1)S(1)}, bf16[4,32,4096]{2,1,0:T(8,128)(2,1)}, u32[]{:S(2)}) copy-start(bf16[4,32,4096]{2,1,0:T(8,128)(2,1)} %all-gather.8.cloned.1.call-done) | copy-start | bytes 3145732
  110.1 294.4 %collective-permute-start.2 = (bf16[1024,1024]{1,0:T(8,128)(2,1)}, bf16[1024,1024]{1,0:T(8,128)(2,1)}, u32[]{:S(2)}, u32[]{:S(2)}) collective-permute-start(bf16[1024,1024]{1,0:T(8,128)(2,1)} %collective-permute-done.1), channel_id=1, source_target_pairs={{0,4},{4,8},{8,12},{12,0},{1,5},{5,9},{9,13},{13,1},{2,6},{6,10},{... | collective-permute-start | bytes 6291464 | tf_op jit(solution)/shard_map/ppermute | solution.py:62
  365.0 70.2 %reduce-scatter.5.cloned.1.call-start = ((), (), s32[]{:S(2)}) async-start(), calls=%async_computation.7 | async-start | bytes 1310720 | tf_op jit(solution)/shard_map/reduce_scatter | solution.py:70
  398.4 1.6 copy-start.4
  404.5 30.7 %copy-start.2 = (bf16[4,32,1024]{2,1,0:T(8,128)(2,1)S(1)}, bf16[4,32,1024]{2,1,0:T(8,128)(2,1)}, u32[]{:S(2)}) copy-start(bf16[4,32,1024]{2,1,0:T(8,128)(2,1)} %reduce-scatter.3.cloned.1.call-done) | copy-start | bytes 786436
  406.6 1.0 copy-start.1
Sparse Core Ops, SparseCore 0:
  20.0 27.4 reduce-scatter.2
  49.1 27.9 all-gather.7
  78.7 181.4 all-gather.3
  261.7 80.7 all-gather.5
  365.1 31.8 all-reduce.1
  407.8 27.3 reduce-scatter.4
